TPU v7x, 32 devices: a whole 2x2x4 slice. The times are simulated.
32 devices in a mesh: gx: 2 (over x), gy: 4 (over z), gz: 4 (over y, core).
Axes of the slice: x: 2, y: 2, z: 4, core: 2. Of those that a mesh axis runs over, the one named last changes fastest.
Arguments:
- order_parameter: float32 [8, 512, 512], P('gx', 'gy', 'gz'), may hold values from -1 to 1
- dissolved_species: float32 [8, 512, 512], P('gx', 'gy', 'gz'), may hold values from -0.8 to 0.2
- broad_undercool: float32 [128, 128, 2], P('gy', 'gz'), may hold values from -2.4 to 2.4
Outputs:
- phase_out: float32 [8, 512, 512], P('gx', 'gy', 'gz')
- solute_out: float32 [8, 512, 512], P('gx', 'gy', 'gz')
- temperature_out: float32 [128, 128, 2], P('gy', 'gz')
All inputs are finite; a program needn't handle non-finite values.
Results may differ from a plain program's by a relative error of at most 0.0001.
Values sent between devices are 32-bit elements; how exact they have to be, the bound alone decides.
No kernel may reach another device: no remote copies, remote signals or barrier semaphores. Data moves between devices by JAX's collectives and lax.ppermute only.
A program may use at most 64 MiB of HBM per device.

v0:
```python
import jax
import jax.numpy as jnp
from jax import lax
from jax.experimental import pallas as pl
from jax.experimental.pallas import tpu as pltpu
from jax.sharding import PartitionSpec as P


FACTOR = 4
SUBSTEPS = 4

TIME_INCREMENT = 0.1
COUPLING = 3.0
PARTITION = 0.3
DIFFUSION = 1.0
THERMAL_SPREAD = 1.2
FREEZING_WARMTH = 2.0

LANES = 128
ROWS = 8
HALO = FACTOR * SUBSTEPS
BANDS = 4
SLOT = 2 * HALO
REACH_P = HALO - FACTOR + 1
REACH_U = HALO - FACTOR
SMALL_VMEM = 4 << 20
STEP_VMEM = 24 << 20


def padded_2(cells, sides, width):
    for axis, dim in sides:
        count = lax.axis_size(axis)
        head = lax.slice_in_dim(cells, 0, width, axis=dim)
        tail = lax.slice_in_dim(cells, cells.shape[dim] - width, cells.shape[dim], axis=dim)
        cells = jnp.concatenate(
            [
                lax.ppermute(tail, axis, [(i, (i + 1) % count) for i in range(count)]),
                cells,
                lax.ppermute(head, axis, [((i + 1) % count, i) for i in range(count)]),
            ],
            axis=dim,
        )
    return cells


def laplace_padded(padded):
    center = padded[1:-1, 1:-1, 1:-1]
    total = padded[2:, 1:-1, 1:-1] + padded[:-2, 1:-1, 1:-1]
    total = total + padded[1:-1, 2:, 1:-1] + padded[1:-1, :-2, 1:-1]
    total = total + padded[1:-1, 1:-1, 2:] + padded[1:-1, 1:-1, :-2]
    return total - 6.0 * center


def flux_padded(values, mobility):
    center_v = values[1:-1, 1:-1, 1:-1]
    center_m = mobility[1:-1, 1:-1, 1:-1]
    total = jnp.zeros_like(center_v)
    pairs = (
        (
            values[2:, 1:-1, 1:-1],
            values[:-2, 1:-1, 1:-1],
            mobility[2:, 1:-1, 1:-1],
            mobility[:-2, 1:-1, 1:-1],
        ),
        (
            values[1:-1, 2:, 1:-1],
            values[1:-1, :-2, 1:-1],
            mobility[1:-1, 2:, 1:-1],
            mobility[1:-1, :-2, 1:-1],
        ),
        (
            values[1:-1, 1:-1, 2:],
            values[1:-1, 1:-1, :-2],
            mobility[1:-1, 1:-1, 2:],
            mobility[1:-1, 1:-1, :-2],
        ),
    )
    for upper_v, lower_v, upper_m, lower_m in pairs:
        total = (
            total
            + 0.5 * (upper_m + center_m) * (upper_v - center_v)
            - 0.5 * (center_m + lower_m) * (center_v - lower_v)
        )
    return total


def phase_update(phase_pad, centre_phase, centre_solute, centre_temp):
    square = 1.0 - centre_phase * centre_phase
    driving = (
        laplace_padded(phase_pad)
        + centre_phase
        - centre_phase * centre_phase * centre_phase
        - COUPLING * square * square * (centre_solute + centre_temp)
    )
    return jnp.clip(centre_phase + TIME_INCREMENT * driving, -1.0, 1.0)


def stepwise(order_parameter, dissolved_species, broad_undercool):
    size_x, size_y, size_z = order_parameter.shape
    coarse_x = size_x // FACTOR
    coarse_y = size_y // FACTOR
    coarse_z = size_z // FACTOR
    start_x = lax.axis_index("gx") * coarse_x
    own_block = lax.dynamic_slice_in_dim(broad_undercool, start_x, coarse_x, 2)
    for _ in range(SUBSTEPS):
        planes = own_block
        local_col = jnp.transpose(planes, (2, 0, 1))
        fine_temp = jnp.repeat(jnp.repeat(jnp.repeat(local_col, FACTOR, 0), FACTOR, 1), FACTOR, 2)
        stacked = jnp.stack([order_parameter, dissolved_species])
        padded = padded_2(stacked, (("gx", 1), ("gy", 2), ("gz", 3)), 1)
        solute_pad = padded[1]
        new_phase = phase_update(padded[0], order_parameter, dissolved_species, fine_temp)
        new_pad = padded_2(new_phase, (("gx", 0), ("gy", 1), ("gz", 2)), 1)
        mobility = 0.5 * (1.0 - new_pad)
        change = new_phase - order_parameter
        numer = (
            TIME_INCREMENT * DIFFUSION * flux_padded(solute_pad, mobility)
            + 0.5 * (1.0 + (1.0 - PARTITION) * dissolved_species) * change
        )
        new_solute = dissolved_species + numer / (
            0.5 * (1.0 + PARTITION - (1.0 - PARTITION) * new_phase)
        )
        blocks = (0.5 * change).reshape(coarse_x, FACTOR, coarse_y, FACTOR, coarse_z, FACTOR)
        freezing_warmth_source = jnp.transpose(jnp.mean(blocks, axis=(1, 3, 5)), (1, 2, 0))
        block_pad = padded_2(own_block, (("gx", 2), ("gy", 0), ("gz", 1)), 1)
        own_block = (
            own_block
            + TIME_INCREMENT * THERMAL_SPREAD * laplace_padded(block_pad)
            + FREEZING_WARMTH * freezing_warmth_source
        )
        order_parameter = new_phase
        dissolved_species = new_solute
    vertical_pile = lax.all_gather(own_block, "gx", axis=2, tiled=True)
    return (order_parameter, dissolved_species, vertical_pile)


def lane_index(shape):
    return lax.broadcasted_iota(jnp.int32, shape, 1)


def turn(tile, shift):
    shift = shift % LANES
    return tile if shift == 0 else pltpu.roll(tile, shift, 1)


def choose(pairs, shape, width):
    group = lane_index(shape) // width
    out = pairs[0][1]
    for index, tile in pairs[1:]:
        out = jnp.where(group == index, tile, out)
    return out


def spread_matrix(rows, cols, by_row):
    i = lax.broadcasted_iota(jnp.int32, (rows, cols), 0)
    j = lax.broadcasted_iota(jnp.int32, (rows, cols), 1)
    same = (i // FACTOR == j) if by_row else (i == j // FACTOR)
    return same.astype(jnp.float32)


def pick_matrix(rows, cols, by_row):
    i = lax.broadcasted_iota(jnp.int32, (rows, cols), 0)
    j = lax.broadcasted_iota(jnp.int32, (rows, cols), 1)
    same = (j == i * FACTOR) if by_row else (i == j * FACTOR)
    return same.astype(jnp.float32)


def exact_dot(a, b):
    return jnp.dot(a, b, precision=lax.Precision.HIGHEST, preferred_element_type=jnp.float32)


def pool_lanes(v):
    i = lax.broadcasted_iota(jnp.int32, (LANES, LANES), 0)
    j = lax.broadcasted_iota(jnp.int32, (LANES, LANES), 1)
    same = (i // FACTOR == j // FACTOR).astype(jnp.float32).astype(jnp.bfloat16)
    total = None
    for _ in range(3):
        part = v.astype(jnp.bfloat16)
        v = v - part.astype(jnp.float32)
        term = jnp.dot(part, same, preferred_element_type=jnp.float32)
        total = term if total is None else total + term
    return total


def pack_kernel(me_ref, p_hbm, u_hbm, t_hbm, zlo, zhi, tf_ref, p_ref, u_ref, t_ref, sems):
    size_x, size_y, _ = p_ref.shape
    pairs = ((t_hbm, t_ref), (p_hbm, p_ref), (u_hbm, u_ref))
    copies = [pltpu.make_async_copy(src, dst, sems.at[i]) for i, (src, dst) in enumerate(pairs)]
    for copy in copies:
        copy.start()
    copies[0].wait()
    first = me_ref[0] == 0
    long = spread_matrix(t_ref.shape[2], LANES, False)
    layers = exact_dot(jnp.concatenate([t_ref[:, g, :] for g in range(2)], 0), long)
    count = t_ref.shape[0]
    layers = [layers[count * g : count * g + count] for g in range(2)]
    for g in range(2):
        layer = jnp.where(first, layers[g], layers[1 - g])
        for j in range(FACTOR):
            tf_ref[g, pl.ds(j, count, stride=FACTOR), :] = layer
    shape = (HALO, LANES)
    parts = size_y // HALO

    def strips(ref, at):
        for i in range(ref.shape[0]):
            rows = [ref[i, pl.ds(HALO * g, HALO), :] for g in range(parts)]
            zlo[at + i] = choose([(g, turn(rows[g], HALO * g)) for g in range(parts)], shape, HALO)
            zhi[at + i] = choose([(g, turn(rows[g], HALO * g + HALO)) for g in range(parts)], shape, HALO)

    strips(tf_ref, 2 * size_x)
    copies[1].wait()
    strips(p_ref, 0)
    copies[2].wait()
    strips(u_ref, size_x)


def band_shape(size_y):
    tall = size_y + 2 * HALO
    return tall // BANDS, BANDS * tall // LANES


def side_kernel(p_ref, u_ref, tf_ref, zlo, zhi, side, side_t, ylo, yhi):
    size_x, size_y, _ = p_ref.shape
    band, _ = band_shape(size_y)
    shape = (ROWS, LANES)
    fields = 2 * size_x
    for f in range(fields + 2):
        out = side.at[f] if f < fields else side_t.at[f - fields]
        for r in range(0, band, ROWS):
            pairs = []
            for b in range(BANDS):
                y = band * b + r - HALO
                if 0 <= y < size_y:
                    j, sub = divmod(y, HALO)
                    rows = pl.ds(sub, ROWS)
                    pairs.append((2 * b, turn(zlo[f, rows, :], SLOT * b - HALO * j)))
                    pairs.append((2 * b + 1, turn(zhi[f, rows, :], SLOT * b + HALO - HALO * j)))
            out[pl.ds(r, ROWS), :] = choose(pairs, shape, HALO)
    for out, y, b, below in ((ylo, 0, 0, True), (yhi, size_y, BANDS - 1, False)):
        for field, ref in enumerate((p_ref, u_ref)):
            reach, at = strip_rows(size_x, field, 0)
            first = y if below else y - reach
            r = first + HALO - band * b
            for k in range(size_x):
                out[pl.ds(at + reach * k, reach), :] = ref[k, pl.ds(first, reach), :]
            tiles = [(k, turn(side[field * size_x + k, pl.ds(r, reach), :], SLOT * (k - b))) for k in range(size_x)]
            out[pl.ds(at + reach * size_x, reach), :] = choose(tiles, (reach, LANES), SLOT)
        few = HALO // FACTOR
        _, at = strip_rows(size_x, 2, 0)
        first = y if below else y - HALO
        r = first + HALO - band * b
        for g in range(2):
            out[pl.ds(at + few * g, few), :] = tf_ref[g, pl.ds(first, few, stride=FACTOR), :]
        tiles = [(g, turn(side_t[g, pl.ds(r, few, stride=FACTOR), :], SLOT * (g - b))) for g in range(2)]
        out[pl.ds(at + 2 * few, few), :] = choose(tiles, (few, LANES), SLOT)


def strip_rows(size_x, field, tile):
    reach = (REACH_P, REACH_U, HALO // FACTOR)[field]
    return reach, HALO - REACH_P + (size_x + 1) * sum((REACH_P, REACH_U)[:field]) + reach * tile


def strip_height(size_x):
    rows = strip_rows(size_x, 2, 3)[1]
    return -(-rows // ROWS) * ROWS


def strip_readers(size_x, field, tile, low_ref, high_ref):
    reach, at = strip_rows(size_x, field, tile)

    def low(r):
        return low_ref[pl.ds(at + r - (HALO - reach), ROWS), :]

    def high(r):
        return high_ref[pl.ds(at + r, ROWS), :]

    return low, high


def to_bands(rows_of, halo, tiles):
    lane = lane_index((ROWS, LANES))
    turned = [turn(rows_of(b), HALO + SLOT * b) for b in range(BANDS)]
    out = []
    for t in range(tiles):
        tile = halo
        if t > 0:
            tile = jnp.where(lane < SLOT * t - HALO, turned[t - 1], tile)
        if t < BANDS:
            tile = jnp.where(lane >= SLOT * t + HALO, turned[t], tile)
        out.append(tile)
    return out


def fill_plane(put, core, low, high, side, corner_low, corner_high, slot, size_y):
    band, tiles = band_shape(size_y)
    lane = lane_index((ROWS, LANES))

    for r in range(0, band, ROWS):
        def rows_of(b):
            y = band * b + r - HALO
            return low(r) if y < 0 else high(y - size_y) if y >= size_y else core(y)

        halo = side(r)
        if r < HALO:
            halo = jnp.where(lane < SLOT, turn(corner_low(r), -SLOT * slot), halo)
        if r >= band - HALO:
            halo = jnp.where(lane >= LANES - SLOT, turn(corner_high(r - band + HALO), -SLOT - SLOT * slot), halo)
        for t, tile in enumerate(to_bands(rows_of, halo, tiles)):
            put(t, r, tile)


def along_z(cells, reach):
    lane = lane_index(cells[0].shape)
    tiles = len(cells)
    left = [turn(c, -reach) for c in cells]
    right = [turn(c, reach) for c in cells]
    up = [jnp.where(lane >= LANES - reach, left[t + 1], left[t]) if t + 1 < tiles else left[t] for t in range(tiles)]
    down = [jnp.where(lane < reach, right[t - 1], right[t]) if t > 0 else right[t] for t in range(tiles)]
    return up, down


def keep_shifts(field, up, down, at, some):
    tiles = field.shape[1]
    for k in some:
        above, below = along_z([field[k, t, pl.ds(at, ROWS), :] for t in range(tiles)], 1)
        for t in range(tiles):
            up[k, t, pl.ds(at, ROWS), :] = above[t]
            down[k, t, pl.ds(at, ROWS), :] = below[t]


def join_bands(field, some, rows):
    _, tiles, height, _ = field.shape
    flat = field.reshape(field.shape[0] * tiles * height, LANES)
    lane = lane_index((len(some), LANES))

    def row_of_planes(t, i):
        return pl.ds((some[0] * tiles + t) * height + i, len(some), stride=tiles * height)

    last = [turn(flat[row_of_planes(t, ROWS + rows - 1), :], SLOT) for t in range(tiles)]
    start = [turn(flat[row_of_planes(t, ROWS), :], -SLOT) for t in range(tiles)]
    for t in range(tiles):
        if t > 0:
            tile = last[t - 1] if t == 1 else jnp.where(lane >= SLOT, last[t - 1], last[t - 2])
            flat[row_of_planes(t, ROWS - 1), :] = tile
        if t + 1 < tiles:
            tile = start[t + 1] if t + 2 == tiles else jnp.where(lane < LANES - SLOT, start[t + 1], start[t + 2])
            flat[row_of_planes(t, ROWS + rows), :] = tile


def sweep(rows, work, follow=None, lead=None):
    if lead is not None:
        lead(ROWS)

    def body(i, _):
        at = pl.multiple_of(ROWS + i * ROWS, ROWS)
        if lead is not None:
            lead(at + ROWS)
        if follow is not None:
            follow(at - ROWS)
        work(at)

    lax.fori_loop(0, rows // ROWS, body, None)
    if follow is not None:
        follow(rows)


def own_kernel(p_ref, u_ref, tf_ref, side, side_t, ylo, yhi, p_own, u_own, p_up, p_down, u_up, u_down, warm, small):
    size_x, size_y, _ = p_ref.shape
    band, tiles = band_shape(size_y)
    few = band // FACTOR
    row = lax.broadcasted_iota(jnp.int32, (ROWS, LANES), 0)
    for field, (dst, core) in enumerate(((p_own, p_ref), (u_own, u_ref))):
        for k in range(size_x):
            f = field * size_x + k

            def put(t, r, tile):
                dst[k, t, pl.ds(ROWS + r, ROWS), :] = tile

            rows = strip_readers(size_x, field, k, ylo, yhi)
            corners = strip_readers(size_x, field, size_x, ylo, yhi)
            fill_plane(
                put, lambda y: core[k, pl.ds(y, ROWS), :], *rows, lambda r: side[f, pl.ds(r, ROWS), :], *corners, k, size_y
            )

    def spread(ref, part, r):
        at = strip_rows(size_x, 2, part)[1] + r // FACTOR
        return jnp.where(row < FACTOR, ref[pl.ds(at, 1), :], ref[pl.ds(at + 1, 1), :])

    for g in range(2):
        def put(t, r, tile):
            warm[g, t, pl.ds(r, ROWS), :] = tile

        fill_plane(
            put, lambda y: tf_ref[g, pl.ds(y, ROWS), :],
            lambda r: spread(ylo, g, r), lambda r: spread(yhi, g, r),
            lambda r: side_t[g, pl.ds(r, ROWS), :],
            lambda r: spread(ylo, 2, r), lambda r: spread(yhi, 2, r),
            g, size_y,
        )
        for t in range(tiles):
            small[g, t, pl.ds(ROWS, few), :] = warm[g, t, pl.ds(0, few, stride=FACTOR), :]
    own = range(size_x)

    def shifts(at):
        keep_shifts(p_own, p_up, p_down, at, own)
        keep_shifts(u_own, u_up, u_down, at, own)

    sweep(band, shifts)
    join_bands(p_own, own, band)
    join_bands(u_own, own, band)
    join_bands(small, range(2), few)


def step_kernel(
    me_ref, pp_ref, up_ref, side, ylo, yhi, p_own, u_own, p_up_own, p_down_own, u_up_own, u_down_own, warm_own, small_own,
    po_ref, uo_ref, to_ref,
    p0, p1, u0, u1, around, p_up, p_down, u_up, u_down, warm, heats, k0, k1, flat,
):
    size_x, size_y, _ = pp_ref.shape
    planes = 2 * size_x
    band, tiles = band_shape(size_y)
    shape = (ROWS, LANES)
    lane = lane_index(shape)
    few = band // FACTOR
    every = range(tiles)
    everything, own, others = range(planes), range(size_x), range(size_x, planes)

    def of_planes(mine, ref):
        return [mine.at[k] for k in own] + [ref.at[k] for k in others]

    def all_of(ref):
        return [ref.at[k] for k in everything]

    phase = [of_planes(p_own, p0), all_of(p1), all_of(p0)]
    solute = [of_planes(u_own, u0), all_of(u1), all_of(u0)]
    first_p_up, first_p_down = of_planes(p_up_own, p_up), of_planes(p_down_own, p_down)
    first_u_up, first_u_down = of_planes(u_up_own, u_up), of_planes(u_down_own, u_down)

    def at_step(states, step):
        return states[0] if step == 0 else states[2 - step % 2]

    for field, (dst, core) in enumerate(((p0, pp_ref), (u0, up_ref))):
        for k in range(size_x):
            f = field * size_x + k

            def put(t, r, tile):
                dst[size_x + k, t, pl.ds(ROWS + r, ROWS), :] = tile

            rows = strip_readers(size_x, field, k, ylo, yhi)
            corners = strip_readers(size_x, field, size_x, ylo, yhi)
            fill_plane(
                put, lambda y: core[k, pl.ds(y, ROWS), :], *rows, lambda r: side[f, pl.ds(r, ROWS), :], *corners, k, size_y
            )

    def new_value(c, total, drive):
        c2 = c * c
        square = 1.0 - c2
        driving = total - c * (5.0 + c2) - (COUPLING * square * square) * drive
        return jnp.clip(c + TIME_INCREMENT * driving, -1.0, 1.0)

    def phase_pass(step, kept):
        pa, pb, ua = at_step(phase, step), p0 if step % 2 else p1, at_step(solute, step)
        temperatures = warm_own if step == 0 else warm

        def work(at):
            here, above, below = pl.ds(at, ROWS), pl.ds(at + 1, ROWS), pl.ds(at - 1, ROWS)
            plain = pl.ds(at - ROWS, ROWS)
            for g in range(2):
                for t in every:
                    heat = None
                    temperature = temperatures[g, t, plain, :]
                    for k in range(g * size_x, (g + 1) * size_x):
                        old = pa[k][t, here, :]
                        if step == 0:
                            total = pa[(k + 1) % planes][t, here, :] + pa[(k - 1) % planes][t, here, :]
                            total = total + pa[k][t, above, :] + pa[k][t, below, :]
                            total = total + first_p_up[k][t, here, :] + first_p_down[k][t, here, :]
                        else:
                            total = around[k, t, here, :]
                        new = new_value(old, total, ua[k][t, here, :] + temperature)
                        pb[k, t, here, :] = new
                        heat = new - old if heat is None else heat + (new - old)
                    heats[g, t, plain, :] = heat

        sweep(band, work)
        join_bands(pb, kept, band)

    def temperature_pass(step, last):
        ka, kb = small_own if step == 0 else k0 if step % 2 == 0 else k1, k0 if step % 2 else k1
        scale = FREEZING_WARMTH * 0.5 / FACTOR**3
        conduct = TIME_INCREMENT * THERMAL_SPREAD
        tiles_of = [(g, r, t) for g in range(2) for r in range(0, few, ROWS) for t in every]
        sources = [
            sum(heats[g, t, pl.ds(FACTOR * r + j, ROWS, stride=FACTOR), :] for j in range(FACTOR)) for g, r, t in tiles_of
        ]
        pooled = pool_lanes(jnp.concatenate(sources, 0))
        pooled = {key: pooled[ROWS * i : ROWS * i + ROWS] for i, key in enumerate(tiles_of)}
        for g in range(2):
            for r in range(0, few, ROWS):
                count = min(ROWS, few - r)
                at = pl.ds(ROWS + r, ROWS)
                far, near = pl.ds(ROWS + r + 1, ROWS), pl.ds(ROWS + r - 1, ROWS)
                up, down = along_z([ka[g, t, at, :] for t in every], FACTOR)
                for t in every:
                    mine = ka[g, t, at, :]
                    total = 2.0 * ka[1 - g, t, at, :] + up[t] + down[t] + ka[g, t, far, :] + ka[g, t, near, :]
                    new = mine + conduct * (total - 6.0 * mine) + scale * pooled[g, r, t]
                    kb[g, t, at, :] = new
                    if not last:
                        for j in range(FACTOR):
                            warm[g, t, pl.ds(FACTOR * r + j, count, stride=FACTOR), :] = new[:count]
        if not last:
            join_bands(kb, range(2), few)

    def solute_pass(step, last):
        pa, pb = at_step(phase, step), p0 if step % 2 else p1
        ua, ub = at_step(solute, step), u0 if step % 2 else u1
        u_above, u_below = (first_u_up, first_u_down) if step == 0 else (all_of(u_up), all_of(u_down))

        def cell(u, p, p_old, near):
            total_u, total_p = near[0]
            total_w = total_u * total_p
            for un, pn in near[1:]:
                total_u, total_p, total_w = total_u + un, total_p + pn, total_w + un * pn
            flux = (2.0 - p) * (total_u - 6.0 * u) + u * total_p - total_w
            part = 0.5 * (1.0 - PARTITION)
            numer = (0.25 * TIME_INCREMENT * DIFFUSION / part) * flux + (u + 0.5 / part) * (p - p_old)
            return u + numer / (0.5 * (1.0 + PARTITION) / part - p), total_p

        def work(at):
            here, above, below = pl.ds(at, ROWS), pl.ds(at + 1, ROWS), pl.ds(at - 1, ROWS)
            for t in every:
                for k in range(size_x if last else planes):
                    pick = lambda i, w: (ua[i % planes][t, w, :], pb[i % planes, t, w, :])
                    near = [pick(k + 1, here), pick(k - 1, here), pick(k, above), pick(k, below)]
                    near += [(u_above[k][t, here, :], p_up[k, t, here, :]), (u_below[k][t, here, :], p_down[k, t, here, :])]
                    u, p = pick(k, here)
                    new, total = cell(u, p, pa[k][t, here, :], near)
                    ub[k, t, here, :] = new
                    if not last:
                        around[k, t, here, :] = total

        kept = own if last else everything
        follow = None if last else lambda at: keep_shifts(ub, u_up, u_down, at, everything)
        sweep(band, work, follow, lambda at: keep_shifts(pb, p_up, p_down, at, kept))
        if not last:
            join_bands(ub, everything, band)

    def first_shifts(at):
        keep_shifts(p0, p_up, p_down, at, others)
        keep_shifts(u0, u_up, u_down, at, others)

    sweep(band, first_shifts)
    join_bands(p0, others, band)
    join_bands(u0, others, band)
    for step in range(SUBSTEPS):
        last = step == SUBSTEPS - 1
        phase_pass(step, own if last else everything)
        temperature_pass(step, last)
        solute_pass(step, last)

    def from_bands(tile_of, b):
        at = HALO + SLOT * b
        return turn(jnp.where(lane_index(tile_of(b).shape) >= at, tile_of(b), tile_of(b + 1)), -at)

    for src, out in (((p1, p0)[SUBSTEPS % 2 == 0], po_ref), ((u1, u0)[SUBSTEPS % 2 == 0], uo_ref)):
        for k in own:
            for r in range(0, band, ROWS):
                for b in range(BANDS):
                    y = band * b + r - HALO
                    if 0 <= y < size_y:
                        out[k, pl.ds(y, ROWS), :] = from_bands(lambda t: src[k, t, pl.ds(ROWS + r, ROWS), :], b)
    first = me_ref[0] == 0
    short = pick_matrix(LANES, to_ref.shape[2], False)
    last = (k1, k0)[SUBSTEPS % 2 == 0]
    layers = []
    for g in range(2):
        for b in range(BANDS):
            flat[g, pl.ds(ROWS + few * b - HALO // FACTOR, 2 * ROWS), :] = from_bands(lambda t: last[g, t, pl.ds(ROWS, 2 * ROWS), :], b)
        layers.append(exact_dot(flat[g, pl.ds(ROWS, to_ref.shape[0]), :], short))
    for g in range(2):
        to_ref[:, g, :] = jnp.where(first, layers[g], layers[1 - g])


def shifted(x, axis, step):
    count = lax.axis_size(axis)
    return lax.ppermute(x, axis, [(i, (i + step) % count) for i in range(count)])


def swapped(x):
    return lax.ppermute(x, "gx", [(0, 1), (1, 0)])


def at_once(order_parameter, dissolved_species, broad_undercool):
    size_x, size_y, size_z = order_parameter.shape
    f32 = jnp.float32
    planes = 2 * size_x
    me = lax.axis_index("gx").astype(jnp.int32).reshape(1)
    coarse = jnp.transpose(broad_undercool, (0, 2, 1))
    smem = pl.BlockSpec(memory_space=pltpu.SMEM)
    vmem = pl.BlockSpec(memory_space=pltpu.VMEM)
    shape = jax.ShapeDtypeStruct
    band, tiles = band_shape(size_y)
    small = pltpu.CompilerParams(vmem_limit_bytes=SMALL_VMEM)

    partner_p = swapped(order_parameter)
    partner_u = swapped(dissolved_species)

    strip = shape((planes + 2, HALO, LANES), f32)
    to_low, to_high, fine = pl.pallas_call(
        pack_kernel,
        out_shape=[strip] * 2 + [shape((2, size_y, size_z), f32)],
        in_specs=[smem] + [pl.BlockSpec(memory_space=pltpu.HBM)] * 3,
        out_specs=[vmem] * 3,
        scratch_shapes=[pltpu.VMEM(x.shape, f32) for x in (order_parameter, dissolved_species, coarse)]
        + [pltpu.SemaphoreType.DMA((3,))],
        compiler_params=small,
        name="pack",
    )(me, *(pltpu.with_memory_space_constraint(x, pltpu.HBM) for x in (order_parameter, dissolved_species, coarse)))
    zhi = shifted(to_low, "gz", -1)
    zlo = shifted(to_high, "gz", 1)
    strip = shape((strip_height(size_x), LANES), f32)
    side, side_t, to_low, to_high = pl.pallas_call(
        side_kernel,
        out_shape=[shape((planes, band, LANES), f32), shape((2, band, LANES), f32), strip, strip],
        in_specs=[vmem] * 5,
        out_specs=[vmem] * 4,
        compiler_params=small,
        name="side",
    )(order_parameter, dissolved_species, fine, zlo, zhi)
    side_other = swapped(side)
    yhi = shifted(to_low, "gy", -1)
    ylo = shifted(to_high, "gy", 1)
    yhi_other = swapped(yhi)
    ylo_other = swapped(ylo)

    rows = band + 2 * ROWS
    cells, warm = (planes, tiles, rows, LANES), (2, tiles, rows + ROWS, LANES)
    mine = pl.pallas_call(
        own_kernel,
        out_shape=[shape((size_x, *cells[1:]), f32)] * 6 + [shape(warm, f32)] * 2,
        in_specs=[vmem] * 7,
        out_specs=[vmem] * 8,
        compiler_params=pltpu.CompilerParams(vmem_limit_bytes=2 * SMALL_VMEM),
        name="own",
    )(order_parameter, dissolved_species, fine, side, side_t, ylo, yhi)
    flat = pltpu.VMEM((2, size_y // FACTOR + 3 * ROWS, LANES), f32)
    new_p, new_u, new_t = pl.pallas_call(
        step_kernel,
        out_shape=[shape(order_parameter.shape, f32), shape(dissolved_species.shape, f32), shape(coarse.shape, f32)],
        in_specs=[smem] + [vmem] * 13,
        out_specs=[vmem] * 3,
        scratch_shapes=[pltpu.VMEM(cells, f32)] * 9 + [pltpu.VMEM(warm, f32)] * 4 + [flat],
        compiler_params=pltpu.CompilerParams(vmem_limit_bytes=STEP_VMEM),
        name="steps",
    )(me, partner_p, partner_u, side_other, ylo_other, yhi_other, *mine)
    return new_p, new_u, jnp.transpose(new_t, (0, 2, 1))


def per_device(order_parameter, dissolved_species, broad_undercool):
    size_x, size_y, size_z = order_parameter.shape
    whole_x = lax.axis_size("gx") == 2 and broad_undercool.shape[2] * FACTOR == 2 * size_x
    if whole_x and size_x == FACTOR == BANDS and size_y == size_z == LANES == SLOT * BANDS:
        return at_once(order_parameter, dissolved_species, broad_undercool)
    return stepwise(order_parameter, dissolved_species, broad_undercool)


def solution(mesh):
    return jax.shard_map(
        per_device,
        mesh=mesh,
        in_specs=(P("gx", "gy", "gz"), P("gx", "gy", "gz"), P("gy", "gz", None)),
        out_specs=(P("gx", "gy", "gz"), P("gx", "gy", "gz"), P("gy", "gz", None)),
        check_vma=False,
    )
```

profile of v0, /device:TPU:0, one launch (start us, length us, event | category | flops | bytes accessed | tf_op | source)
XLA Modules:
  0.0 35.6 jit_solution(17423709208866063071)
XLA Ops:
  0.6 3.0 %collective-permute-start = (f32[4,128,128]{2,1,0:T(8,128)}, f32[4,128,128]{2,1,0:T(8,128)S(1)}, u32[]{:S(2)}, u32[]{:S(2)}) collective-permute-start(f32[4,128,128]{2,1,0:T(8,128)} %p_ref.3), channel_id=1, source_target_pairs={{0,16},{16,0},{1,17},{17,1},{2,18},{18,2},{3,19},{19,3},{4,20},{20... | collective-permute-start | bytes 786440 | tf_op jit(solution)/shard_map/ppermute | solution.py:591
  3.7 0.1 collective-permute-start.1
  3.7 0.0 copy-start
  3.7 0.0 copy-start.1
  3.7 1.5 %pack.1 = (f32[10,16,128]{2,1,0:T(8,128)S(1)}, f32[10,16,128]{2,1,0:T(8,128)S(1)}, f32[2,128,128]{2,1,0:T(8,128)S(1)}) custom-call(s32[1]{0:T(128)} %bitcast.me_ref, f32[4,128,128]{2,1,0:T(8,128)} %p_ref.3, f32[4,128,128]{2,1,0:T(8,128)} %u_ref.3, f32[32,2,32]{2,1,0:T(2,128)} %bitcast.3), custom_call_target="tpu_custom_call" | custom-call | tf_op jit(solution)/shard_map/pack/pallas_call | solution.py:610
  5.3 0.1 collective-permute-start.2
  5.3 1.7 %collective-permute-start.3 = (f32[10,16,128]{2,1,0:T(8,128)S(1)}, f32[10,16,128]{2,1,0:T(8,128)S(1)}, u32[]{:S(2)}, u32[]{:S(2)}) collective-permute-start(f32[10,16,128]{2,1,0:T(8,128)S(1)} %get-tuple-element.23), channel_id=1, source_target_pairs={{0,3},{1,0},{2,1},{3,2},{4,7},{5,4},{6,5},{7,6},{8,11},{9,8},{10,9... | collective-permute-start | bytes 245768 | tf_op jit(solution)/shard_map/ppermute | solution.py:587
  7.1 2.1 %collective-permute-done.2.zlo = f32[10,16,128]{2,1,0:T(8,128)S(1)} collective-permute-done((f32[10,16,128]{2,1,0:T(8,128)S(1)}, f32[10,16,128]{2,1,0:T(8,128)S(1)}, u32[]{:S(2)}, u32[]{:S(2)}) %collective-permute-start.2) | collective-permute-done | bytes 81952 | tf_op jit(solution)/shard_map/ppermute | solution.py:587
  9.2 0.4 %collective-permute-done.3.zhi = f32[10,16,128]{2,1,0:T(8,128)S(1)} collective-permute-done((f32[10,16,128]{2,1,0:T(8,128)S(1)}, f32[10,16,128]{2,1,0:T(8,128)S(1)}, u32[]{:S(2)}, u32[]{:S(2)}) %collective-permute-start.3) | collective-permute-done | bytes 81952 | tf_op jit(solution)/shard_map/ppermute | solution.py:587
  9.6 0.0 copy-done
  9.6 0.0 copy-done.1
  9.6 0.3 side.1
  9.9 1.6 %collective-permute-start.4 = (f32[8,40,128]{2,1,0:T(8,128)S(1)}, f32[8,40,128]{2,1,0:T(8,128)S(1)}, u32[]{:S(2)}, u32[]{:S(2)}) collective-permute-start(f32[8,40,128]{2,1,0:T(8,128)S(1)} %get-tuple-element.24.side), channel_id=1, source_target_pairs={{0,16},{16,0},{1,17},{17,1},{2,18},{18,2},{3,19},{19,3},{4,20},{20... | collective-permute-start | bytes 491528 | tf_op jit(solution)/shard_map/ppermute | solution.py:591
  11.5 1.6 %collective-permute-start.5 = (f32[144,128]{1,0:T(8,128)S(1)}, f32[144,128]{1,0:T(8,128)S(1)}, u32[]{:S(2)}, u32[]{:S(2)}) collective-permute-start(f32[144,128]{1,0:T(8,128)S(1)} %get-tuple-element.25), channel_id=1, source_target_pairs={{0,4},{4,8},{8,12},{12,0},{1,5},{5,9},{9,13},{13,1},{2,6},{6,10},{... | collective-permute-start | bytes 221192 | tf_op jit(solution)/shard_map/ppermute | solution.py:587
  13.1 2.2 %collective-permute-start.7 = (f32[144,128]{1,0:T(8,128)S(1)}, f32[144,128]{1,0:T(8,128)S(1)}, u32[]{:S(2)}, u32[]{:S(2)}) collective-permute-start(f32[144,128]{1,0:T(8,128)S(1)} %get-tuple-element.26), channel_id=1, source_target_pairs={{0,12},{4,0},{8,4},{12,8},{1,13},{5,1},{9,5},{13,9},{2,14},{6,2},{... | collective-permute-start | bytes 221192 | tf_op jit(solution)/shard_map/ppermute | solution.py:587
  15.3 2.5 %collective-permute-done.5.ylo = f32[144,128]{1,0:T(8,128)S(1)} collective-permute-done((f32[144,128]{1,0:T(8,128)S(1)}, f32[144,128]{1,0:T(8,128)S(1)}, u32[]{:S(2)}, u32[]{:S(2)}) %collective-permute-start.5) | collective-permute-done | bytes 73760 | tf_op jit(solution)/shard_map/ppermute | solution.py:587
  17.8 0.4 %collective-permute-start.6 = (f32[144,128]{1,0:T(8,128)S(1)}, f32[144,128]{1,0:T(8,128)S(1)}, u32[]{:S(2)}, u32[]{:S(2)}) collective-permute-start(f32[144,128]{1,0:T(8,128)S(1)} %collective-permute-done.5.ylo), channel_id=1, source_target_pairs={{0,16},{16,0},{1,17},{17,1},{2,18},{18,2},{3,19},{19,3},{4,20},{20... | collective-permute-start | bytes 221192 | tf_op jit(solution)/shard_map/ppermute | solution.py:591
  18.2 1.3 %collective-permute-done.7.yhi = f32[144,128]{1,0:T(8,128)S(1)} collective-permute-done((f32[144,128]{1,0:T(8,128)S(1)}, f32[144,128]{1,0:T(8,128)S(1)}, u32[]{:S(2)}, u32[]{:S(2)}) %collective-permute-start.7) | collective-permute-done | bytes 73760 | tf_op jit(solution)/shard_map/ppermute | solution.py:587
  19.5 0.6 %collective-permute-start.8 = (f32[144,128]{1,0:T(8,128)S(1)}, f32[144,128]{1,0:T(8,128)S(1)}, u32[]{:S(2)}, u32[]{:S(2)}) collective-permute-start(f32[144,128]{1,0:T(8,128)S(1)} %collective-permute-done.7.yhi), channel_id=1, source_target_pairs={{0,16},{16,0},{1,17},{17,1},{2,18},{18,2},{3,19},{19,3},{4,20},{20... | collective-permute-start | bytes 221192 | tf_op jit(solution)/shard_map/ppermute | solution.py:591
  20.1 1.1 %own.1 = (f32[4,5,56,128]{3,2,1,0:T(8,128)S(1)}, f32[4,5,56,128]{3,2,1,0:T(8,128)S(1)}, f32[4,5,56,128]{3,2,1,0:T(8,128)S(1)}, f32[4,5,56,128]{3,2,1,0:T(8,128)S...) custom-call(f32[4,128,128]{2,1,0:T(8,128)S(1)} %copy-done, ...), custom_call_target="tpu_custom_call" | custom-call | tf_op jit(solution)/shard_map/own/pallas_call | solution.py:639
  21.3 1.6 %collective-permute-done.6.ylo = f32[144,128]{1,0:T(8,128)S(1)} collective-permute-done((f32[144,128]{1,0:T(8,128)S(1)}, f32[144,128]{1,0:T(8,128)S(1)}, u32[]{:S(2)}, u32[]{:S(2)}) %collective-permute-start.6) | collective-permute-done | bytes 73760 | tf_op jit(solution)/shard_map/ppermute | solution.py:591
  22.9 1.3 %collective-permute-done.8.yhi = f32[144,128]{1,0:T(8,128)S(1)} collective-permute-done((f32[144,128]{1,0:T(8,128)S(1)}, f32[144,128]{1,0:T(8,128)S(1)}, u32[]{:S(2)}, u32[]{:S(2)}) %collective-permute-start.8) | collective-permute-done | bytes 73760 | tf_op jit(solution)/shard_map/ppermute | solution.py:591
  24.1 0.0 collective-permute-done.4.side
  24.1 0.0 collective-permute-done.pp_ref
  24.1 0.0 collective-permute-done.1.up_ref
  24.1 11.5 %steps.1 = (f32[4,128,128]{2,1,0:T(8,128)}, f32[4,128,128]{2,1,0:T(8,128)}, f32[32,2,32]{2,1,0:T(2,128)}) custom-call(s32[1]{0:T(128)} %bitcast.me_ref, f32[4,128,128]{2,1,0:T(8,128)S(1)} %collective-permute-done.pp_ref, f32[4,128,128]{2,1,0:T(8,128)S(1)} %collective-permute-done.1.up_ref, f32[8,40,128]{2,1,0:T(8,128)S(1)} %collective-permute-done.4.side, ...), custom_call_target="tpu_custom_call" | custom-call | tf_op jit(solution)/shard_map/steps/pallas_call | solution.py:648
Async XLA Ops:
  0.6 23.5 %collective-permute-start = (f32[4,128,128]{2,1,0:T(8,128)}, f32[4,128,128]{2,1,0:T(8,128)S(1)}, u32[]{:S(2)}, u32[]{:S(2)}) collective-permute-start(f32[4,128,128]{2,1,0:T(8,128)} %p_ref.3), channel_id=1, source_target_pairs={{0,16},{16,0},{1,17},{17,1},{2,18},{18,2},{3,19},{19,3},{4,20},{20... | collective-permute-start | bytes 786440 | tf_op jit(solution)/shard_map/ppermute | solution.py:591
  3.7 20.5 %collective-permute-start.1 = (f32[4,128,128]{2,1,0:T(8,128)}, f32[4,128,128]{2,1,0:T(8,128)S(1)}, u32[]{:S(2)}, u32[]{:S(2)}) collective-permute-start(f32[4,128,128]{2,1,0:T(8,128)} %u_ref.3), channel_id=1, source_target_pairs={{0,16},{16,0},{1,17},{17,1},{2,18},{18,2},{3,19},{19,3},{4,20},{20... | collective-permute-start | bytes 786440 | tf_op jit(solution)/shard_map/ppermute | solution.py:591
  3.7 5.8 %copy-start = (f32[4,128,128]{2,1,0:T(8,128)S(1)}, f32[4,128,128]{2,1,0:T(8,128)}, u32[]{:S(2)}) copy-start(f32[4,128,128]{2,1,0:T(8,128)} %p_ref.3) | copy-start | bytes 786436
  3.7 5.8 %copy-start.1 = (f32[4,128,128]{2,1,0:T(8,128)S(1)}, f32[4,128,128]{2,1,0:T(8,128)}, u32[]{:S(2)}) copy-start(f32[4,128,128]{2,1,0:T(8,128)} %u_ref.3) | copy-start | bytes 786436
  5.3 3.9 %collective-permute-start.2 = (f32[10,16,128]{2,1,0:T(8,128)S(1)}, f32[10,16,128]{2,1,0:T(8,128)S(1)}, u32[]{:S(2)}, u32[]{:S(2)}) collective-permute-start(f32[10,16,128]{2,1,0:T(8,128)S(1)} %get-tuple-element.22), channel_id=1, source_target_pairs={{0,1},{1,2},{2,3},{3,0},{4,5},{5,6},{6,7},{7,4},{8,9},{9,10},{10,1... | collective-permute-start | bytes 245768 | tf_op jit(solution)/shard_map/ppermute | solution.py:587
  5.3 4.2 %collective-permute-start.3 = (f32[10,16,128]{2,1,0:T(8,128)S(1)}, f32[10,16,128]{2,1,0:T(8,128)S(1)}, u32[]{:S(2)}, u32[]{:S(2)}) collective-permute-start(f32[10,16,128]{2,1,0:T(8,128)S(1)} %get-tuple-element.23), channel_id=1, source_target_pairs={{0,3},{1,0},{2,1},{3,2},{4,7},{5,4},{6,5},{7,6},{8,11},{9,8},{10,9... | collective-permute-start | bytes 245768 | tf_op jit(solution)/shard_map/ppermute | solution.py:587
  9.9 14.3 %collective-permute-start.4 = (f32[8,40,128]{2,1,0:T(8,128)S(1)}, f32[8,40,128]{2,1,0:T(8,128)S(1)}, u32[]{:S(2)}, u32[]{:S(2)}) collective-permute-start(f32[8,40,128]{2,1,0:T(8,128)S(1)} %get-tuple-element.24.side), channel_id=1, source_target_pairs={{0,16},{16,0},{1,17},{17,1},{2,18},{18,2},{3,19},{19,3},{4,20},{20... | collective-permute-start | bytes 491528 | tf_op jit(solution)/shard_map/ppermute | solution.py:591
  11.5 6.3 %collective-permute-start.5 = (f32[144,128]{1,0:T(8,128)S(1)}, f32[144,128]{1,0:T(8,128)S(1)}, u32[]{:S(2)}, u32[]{:S(2)}) collective-permute-start(f32[144,128]{1,0:T(8,128)S(1)} %get-tuple-element.25), channel_id=1, source_target_pairs={{0,4},{4,8},{8,12},{12,0},{1,5},{5,9},{9,13},{13,1},{2,6},{6,10},{... | collective-permute-start | bytes 221192 | tf_op jit(solution)/shard_map/ppermute | solution.py:587
  13.1 6.4 %collective-permute-start.7 = (f32[144,128]{1,0:T(8,128)S(1)}, f32[144,128]{1,0:T(8,128)S(1)}, u32[]{:S(2)}, u32[]{:S(2)}) collective-permute-start(f32[144,128]{1,0:T(8,128)S(1)} %get-tuple-element.26), channel_id=1, source_target_pairs={{0,12},{4,0},{8,4},{12,8},{1,13},{5,1},{9,5},{13,9},{2,14},{6,2},{... | collective-permute-start | bytes 221192 | tf_op jit(solution)/shard_map/ppermute | solution.py:587
  17.8 5.0 %collective-permute-start.6 = (f32[144,128]{1,0:T(8,128)S(1)}, f32[144,128]{1,0:T(8,128)S(1)}, u32[]{:S(2)}, u32[]{:S(2)}) collective-permute-start(f32[144,128]{1,0:T(8,128)S(1)} %collective-permute-done.5.ylo), channel_id=1, source_target_pairs={{0,16},{16,0},{1,17},{17,1},{2,18},{18,2},{3,19},{19,3},{4,20},{20... | collective-permute-start | bytes 221192 | tf_op jit(solution)/shard_map/ppermute | solution.py:591
  19.5 4.6 %collective-permute-start.8 = (f32[144,128]{1,0:T(8,128)S(1)}, f32[144,128]{1,0:T(8,128)S(1)}, u32[]{:S(2)}, u32[]{:S(2)}) collective-permute-start(f32[144,128]{1,0:T(8,128)S(1)} %collective-permute-done.7.yhi), channel_id=1, source_target_pairs={{0,16},{16,0},{1,17},{17,1},{2,18},{18,2},{3,19},{19,3},{4,20},{20... | collective-permute-start | bytes 221192 | tf_op jit(solution)/shard_map/ppermute | solution.py:591
where the time goes:
time: 35.8 us; the launch traced here: 35.6 us
  Pallas kernels  14.4 us (40%)
  starting transfers between devices  11.4 us (32%)
  waiting for transfers between devices  9.12 us (25%)
  between operations  0.67 us (2%)
    pallas_call x1, Pallas kernels, at_once(): pl.pallas_call(step_kernel, out_shape=[shape(order_parameter.shape, f32),...  11.5 us
    ppermute x4, waiting for transfers between devices, shifted(): lax.ppermute(x, axis, [(i, (i + step) % count) for i in range(count)])  6.26 us
    ppermute x5, starting transfers between devices, swapped(): return lax.ppermute(x, 'gx', [(0, 1), (1, 0)])  5.76 us
    ppermute x4, starting transfers between devices, shifted(): lax.ppermute(x, axis, [(i, (i + step) % count) for i in range(count)])  5.61 us
    ppermute x5, waiting for transfers between devices, swapped(): return lax.ppermute(x, 'gx', [(0, 1), (1, 0)])  2.87 us
    pallas_call x1, Pallas kernels, at_once(): pl.pallas_call(pack_kernel, out_shape=[strip] * 2 + [shape((2, size_y, si...  1.51 us
    pallas_call x1, Pallas kernels, at_once(): pl.pallas_call(own_kernel, out_shape=[shape((size_x, *cells[1:]), f32)] *...  1.14 us
  transfers between devices with their start and end apart: 9, of which 6 were waited for; matrix products, arithmetic and copies ran while one was open for 0% of the time, Pallas kernels for 8%

commit v1 on v0

--- a/solution.py
+++ b/solution.py
@@ -462,14 +462,15 @@
         pa, pb, ua = at_step(phase, step), p0 if step % 2 else p1, at_step(solute, step)
         temperatures = warm_own if step == 0 else warm
 
-        def work(at):
-            here, above, below = pl.ds(at, ROWS), pl.ds(at + 1, ROWS), pl.ds(at - 1, ROWS)
-            plain = pl.ds(at - ROWS, ROWS)
+        for r in range(0, band, ROWS):
+            at = ROWS + r
+            here, above, below, plain = pl.ds(at, ROWS), pl.ds(at + 1, ROWS), pl.ds(at - 1, ROWS), pl.ds(r, ROWS)
             for g in range(2):
-                for t in every:
-                    heat = None
-                    temperature = temperatures[g, t, plain, :]
-                    for k in range(g * size_x, (g + 1) * size_x):
+                heat = [None] * tiles
+                temperature = [temperatures[g, t, plain, :] for t in every]
+                for k in range(g * size_x, (g + 1) * size_x):
+                    fresh = []
+                    for t in every:
                         old = pa[k][t, here, :]
                         if step == 0:
                             total = pa[(k + 1) % planes][t, here, :] + pa[(k - 1) % planes][t, here, :]
@@ -477,12 +478,17 @@
                             total = total + first_p_up[k][t, here, :] + first_p_down[k][t, here, :]
                         else:
                             total = around[k, t, here, :]
-                        new = new_value(old, total, ua[k][t, here, :] + temperature)
+                        new = new_value(old, total, ua[k][t, here, :] + temperature[t])
                         pb[k, t, here, :] = new
-                        heat = new - old if heat is None else heat + (new - old)
-                    heats[g, t, plain, :] = heat
-
-        sweep(band, work)
+                        heat[t] = new - old if heat[t] is None else heat[t] + (new - old)
+                        fresh.append(new)
+                    if k in kept:
+                        up, down = along_z(fresh, 1)
+                        for t in every:
+                            p_up[k, t, here, :] = up[t]
+                            p_down[k, t, here, :] = down[t]
+                for t in every:
+                    heats[g, t, plain, :] = heat[t]
         join_bands(pb, kept, band)
 
     def temperature_pass(step, last):
@@ -540,9 +546,12 @@
                     if not last:
                         around[k, t, here, :] = total
 
-        kept = own if last else everything
         follow = None if last else lambda at: keep_shifts(ub, u_up, u_down, at, everything)
-        sweep(band, work, follow, lambda at: keep_shifts(pb, p_up, p_down, at, kept))
+        if last:
+            for r in range(0, band, ROWS):
+                work(ROWS + r)
+        else:
+            sweep(band, work, follow)
         if not last:
             join_bands(ub, everything, band)
 

time: 35.8 us -> 33.3 us (0.930)
  Pallas kernels: 14.4 us -> 12 us
    pallas_call x1, Pallas kernels: 11.5 us -> 9.06 us  [at_once(): pl.pallas_call(step_kernel, out_shape=[shape(order_parameter.shape, f32),...]
  transfers between devices with their start and end apart: 9 -> 9, of which waited for: 6 -> 6; matrix products, arithmetic and copies ran while one was open for 0% -> 0% of each run, Pallas kernels for 8% -> 9%
where the time goes in v1:
time: 33.3 us; the launch traced here: 33.2 us
  Pallas kernels  12 us (36%)
  starting transfers between devices  11.4 us (34%)
  waiting for transfers between devices  9.12 us (27%)
  between operations  0.67 us (2%)
    pallas_call x1, Pallas kernels, at_once(): pl.pallas_call(step_kernel, out_shape=[shape(order_parameter.shape, f32),...  9.06 us
    ppermute x4, waiting for transfers between devices, shifted(): lax.ppermute(x, axis, [(i, (i + step) % count) for i in range(count)])  6.26 us
    ppermute x5, starting transfers between devices, swapped(): return lax.ppermute(x, 'gx', [(0, 1), (1, 0)])  5.76 us
    ppermute x4, starting transfers between devices, shifted(): lax.ppermute(x, axis, [(i, (i + step) % count) for i in range(count)])  5.61 us
    ppermute x5, waiting for transfers between devices, swapped(): return lax.ppermute(x, 'gx', [(0, 1), (1, 0)])  2.87 us
    pallas_call x1, Pallas kernels, at_once(): pl.pallas_call(pack_kernel, out_shape=[strip] * 2 + [shape((2, size_y, si...  1.51 us
    pallas_call x1, Pallas kernels, at_once(): pl.pallas_call(own_kernel, out_shape=[shape((size_x, *cells[1:]), f32)] *...  1.14 us
  transfers between devices with their start and end apart: 9, of which 6 were waited for; matrix products, arithmetic and copies ran while one was open for 0% of the time, Pallas kernels for 9%

profile of v1, /device:TPU:0, one launch (start us, length us, event | category | flops | bytes accessed | tf_op | source)
XLA Modules:
  0.0 33.2 jit_solution(8492134067802541471)
XLA Ops:
  0.6 3.0 %collective-permute-start = (f32[4,128,128]{2,1,0:T(8,128)}, f32[4,128,128]{2,1,0:T(8,128)S(1)}, u32[]{:S(2)}, u32[]{:S(2)}) collective-permute-start(f32[4,128,128]{2,1,0:T(8,128)} %p_ref.3), channel_id=1, source_target_pairs={{0,16},{16,0},{1,17},{17,1},{2,18},{18,2},{3,19},{19,3},{4,20},{20... | collective-permute-start | bytes 786440 | tf_op jit(solution)/shard_map/ppermute | solution.py:600
  3.7 0.1 collective-permute-start.1
  3.7 0.0 copy-start
  3.7 0.0 copy-start.1
  3.7 1.5 %pack.1 = (f32[10,16,128]{2,1,0:T(8,128)S(1)}, f32[10,16,128]{2,1,0:T(8,128)S(1)}, f32[2,128,128]{2,1,0:T(8,128)S(1)}) custom-call(s32[1]{0:T(128)} %bitcast.me_ref, f32[4,128,128]{2,1,0:T(8,128)} %p_ref.3, f32[4,128,128]{2,1,0:T(8,128)} %u_ref.3, f32[32,2,32]{2,1,0:T(2,128)} %bitcast.3), custom_call_target="tpu_custom_call" | custom-call | tf_op jit(solution)/shard_map/pack/pallas_call | solution.py:619
  5.3 0.1 collective-permute-start.2
  5.3 1.7 %collective-permute-start.3 = (f32[10,16,128]{2,1,0:T(8,128)S(1)}, f32[10,16,128]{2,1,0:T(8,128)S(1)}, u32[]{:S(2)}, u32[]{:S(2)}) collective-permute-start(f32[10,16,128]{2,1,0:T(8,128)S(1)} %get-tuple-element.23), channel_id=1, source_target_pairs={{0,3},{1,0},{2,1},{3,2},{4,7},{5,4},{6,5},{7,6},{8,11},{9,8},{10,9... | collective-permute-start | bytes 245768 | tf_op jit(solution)/shard_map/ppermute | solution.py:596
  7.1 2.1 %collective-permute-done.2.zlo = f32[10,16,128]{2,1,0:T(8,128)S(1)} collective-permute-done((f32[10,16,128]{2,1,0:T(8,128)S(1)}, f32[10,16,128]{2,1,0:T(8,128)S(1)}, u32[]{:S(2)}, u32[]{:S(2)}) %collective-permute-start.2) | collective-permute-done | bytes 81952 | tf_op jit(solution)/shard_map/ppermute | solution.py:596
  9.2 0.4 %collective-permute-done.3.zhi = f32[10,16,128]{2,1,0:T(8,128)S(1)} collective-permute-done((f32[10,16,128]{2,1,0:T(8,128)S(1)}, f32[10,16,128]{2,1,0:T(8,128)S(1)}, u32[]{:S(2)}, u32[]{:S(2)}) %collective-permute-start.3) | collective-permute-done | bytes 81952 | tf_op jit(solution)/shard_map/ppermute | solution.py:596
  9.6 0.0 copy-done
  9.6 0.0 copy-done.1
  9.6 0.3 side.1
  9.9 1.6 %collective-permute-start.4 = (f32[8,40,128]{2,1,0:T(8,128)S(1)}, f32[8,40,128]{2,1,0:T(8,128)S(1)}, u32[]{:S(2)}, u32[]{:S(2)}) collective-permute-start(f32[8,40,128]{2,1,0:T(8,128)S(1)} %get-tuple-element.24.side), channel_id=1, source_target_pairs={{0,16},{16,0},{1,17},{17,1},{2,18},{18,2},{3,19},{19,3},{4,20},{20... | collective-permute-start | bytes 491528 | tf_op jit(solution)/shard_map/ppermute | solution.py:600
  11.5 1.6 %collective-permute-start.5 = (f32[144,128]{1,0:T(8,128)S(1)}, f32[144,128]{1,0:T(8,128)S(1)}, u32[]{:S(2)}, u32[]{:S(2)}) collective-permute-start(f32[144,128]{1,0:T(8,128)S(1)} %get-tuple-element.25), channel_id=1, source_target_pairs={{0,4},{4,8},{8,12},{12,0},{1,5},{5,9},{9,13},{13,1},{2,6},{6,10},{... | collective-permute-start | bytes 221192 | tf_op jit(solution)/shard_map/ppermute | solution.py:596
  13.1 2.2 %collective-permute-start.7 = (f32[144,128]{1,0:T(8,128)S(1)}, f32[144,128]{1,0:T(8,128)S(1)}, u32[]{:S(2)}, u32[]{:S(2)}) collective-permute-start(f32[144,128]{1,0:T(8,128)S(1)} %get-tuple-element.26), channel_id=1, source_target_pairs={{0,12},{4,0},{8,4},{12,8},{1,13},{5,1},{9,5},{13,9},{2,14},{6,2},{... | collective-permute-start | bytes 221192 | tf_op jit(solution)/shard_map/ppermute | solution.py:596
  15.3 2.5 %collective-permute-done.5.ylo = f32[144,128]{1,0:T(8,128)S(1)} collective-permute-done((f32[144,128]{1,0:T(8,128)S(1)}, f32[144,128]{1,0:T(8,128)S(1)}, u32[]{:S(2)}, u32[]{:S(2)}) %collective-permute-start.5) | collective-permute-done | bytes 73760 | tf_op jit(solution)/shard_map/ppermute | solution.py:596
  17.8 0.4 %collective-permute-start.6 = (f32[144,128]{1,0:T(8,128)S(1)}, f32[144,128]{1,0:T(8,128)S(1)}, u32[]{:S(2)}, u32[]{:S(2)}) collective-permute-start(f32[144,128]{1,0:T(8,128)S(1)} %collective-permute-done.5.ylo), channel_id=1, source_target_pairs={{0,16},{16,0},{1,17},{17,1},{2,18},{18,2},{3,19},{19,3},{4,20},{20... | collective-permute-start | bytes 221192 | tf_op jit(solution)/shard_map/ppermute | solution.py:600
  18.2 1.3 %collective-permute-done.7.yhi = f32[144,128]{1,0:T(8,128)S(1)} collective-permute-done((f32[144,128]{1,0:T(8,128)S(1)}, f32[144,128]{1,0:T(8,128)S(1)}, u32[]{:S(2)}, u32[]{:S(2)}) %collective-permute-start.7) | collective-permute-done | bytes 73760 | tf_op jit(solution)/shard_map/ppermute | solution.py:596
  19.5 0.6 %collective-permute-start.8 = (f32[144,128]{1,0:T(8,128)S(1)}, f32[144,128]{1,0:T(8,128)S(1)}, u32[]{:S(2)}, u32[]{:S(2)}) collective-permute-start(f32[144,128]{1,0:T(8,128)S(1)} %collective-permute-done.7.yhi), channel_id=1, source_target_pairs={{0,16},{16,0},{1,17},{17,1},{2,18},{18,2},{3,19},{19,3},{4,20},{20... | collective-permute-start | bytes 221192 | tf_op jit(solution)/shard_map/ppermute | solution.py:600
  20.1 1.1 %own.1 = (f32[4,5,56,128]{3,2,1,0:T(8,128)S(1)}, f32[4,5,56,128]{3,2,1,0:T(8,128)S(1)}, f32[4,5,56,128]{3,2,1,0:T(8,128)S(1)}, f32[4,5,56,128]{3,2,1,0:T(8,128)S...) custom-call(f32[4,128,128]{2,1,0:T(8,128)S(1)} %copy-done, ...), custom_call_target="tpu_custom_call" | custom-call | tf_op jit(solution)/shard_map/own/pallas_call | solution.py:648
  21.3 1.6 %collective-permute-done.6.ylo = f32[144,128]{1,0:T(8,128)S(1)} collective-permute-done((f32[144,128]{1,0:T(8,128)S(1)}, f32[144,128]{1,0:T(8,128)S(1)}, u32[]{:S(2)}, u32[]{:S(2)}) %collective-permute-start.6) | collective-permute-done | bytes 73760 | tf_op jit(solution)/shard_map/ppermute | solution.py:600
  22.9 1.3 %collective-permute-done.8.yhi = f32[144,128]{1,0:T(8,128)S(1)} collective-permute-done((f32[144,128]{1,0:T(8,128)S(1)}, f32[144,128]{1,0:T(8,128)S(1)}, u32[]{:S(2)}, u32[]{:S(2)}) %collective-permute-start.8) | collective-permute-done | bytes 73760 | tf_op jit(solution)/shard_map/ppermute | solution.py:600
  24.1 0.0 collective-permute-done.4.side
  24.1 0.0 collective-permute-done.pp_ref
  24.1 0.0 collective-permute-done.1.up_ref
  24.1 9.1 %steps.1 = (f32[4,128,128]{2,1,0:T(8,128)}, f32[4,128,128]{2,1,0:T(8,128)}, f32[32,2,32]{2,1,0:T(2,128)}) custom-call(s32[1]{0:T(128)} %bitcast.me_ref, f32[4,128,128]{2,1,0:T(8,128)S(1)} %collective-permute-done.pp_ref, f32[4,128,128]{2,1,0:T(8,128)S(1)} %collective-permute-done.1.up_ref, f32[8,40,128]{2,1,0:T(8,128)S(1)} %collective-permute-done.4.side, ...), custom_call_target="tpu_custom_call" | custom-call | tf_op jit(solution)/shard_map/steps/pallas_call | solution.py:657
Async XLA Ops:
  0.6 23.5 %collective-permute-start = (f32[4,128,128]{2,1,0:T(8,128)}, f32[4,128,128]{2,1,0:T(8,128)S(1)}, u32[]{:S(2)}, u32[]{:S(2)}) collective-permute-start(f32[4,128,128]{2,1,0:T(8,128)} %p_ref.3), channel_id=1, source_target_pairs={{0,16},{16,0},{1,17},{17,1},{2,18},{18,2},{3,19},{19,3},{4,20},{20... | collective-permute-start | bytes 786440 | tf_op jit(solution)/shard_map/ppermute | solution.py:600
  3.7 20.5 %collective-permute-start.1 = (f32[4,128,128]{2,1,0:T(8,128)}, f32[4,128,128]{2,1,0:T(8,128)S(1)}, u32[]{:S(2)}, u32[]{:S(2)}) collective-permute-start(f32[4,128,128]{2,1,0:T(8,128)} %u_ref.3), channel_id=1, source_target_pairs={{0,16},{16,0},{1,17},{17,1},{2,18},{18,2},{3,19},{19,3},{4,20},{20... | collective-permute-start | bytes 786440 | tf_op jit(solution)/shard_map/ppermute | solution.py:600
  3.7 5.8 %copy-start = (f32[4,128,128]{2,1,0:T(8,128)S(1)}, f32[4,128,128]{2,1,0:T(8,128)}, u32[]{:S(2)}) copy-start(f32[4,128,128]{2,1,0:T(8,128)} %p_ref.3) | copy-start | bytes 786436
  3.7 5.8 %copy-start.1 = (f32[4,128,128]{2,1,0:T(8,128)S(1)}, f32[4,128,128]{2,1,0:T(8,128)}, u32[]{:S(2)}) copy-start(f32[4,128,128]{2,1,0:T(8,128)} %u_ref.3) | copy-start | bytes 786436
  5.3 3.9 %collective-permute-start.2 = (f32[10,16,128]{2,1,0:T(8,128)S(1)}, f32[10,16,128]{2,1,0:T(8,128)S(1)}, u32[]{:S(2)}, u32[]{:S(2)}) collective-permute-start(f32[10,16,128]{2,1,0:T(8,128)S(1)} %get-tuple-element.22), channel_id=1, source_target_pairs={{0,1},{1,2},{2,3},{3,0},{4,5},{5,6},{6,7},{7,4},{8,9},{9,10},{10,1... | collective-permute-start | bytes 245768 | tf_op jit(solution)/shard_map/ppermute | solution.py:596
  5.3 4.2 %collective-permute-start.3 = (f32[10,16,128]{2,1,0:T(8,128)S(1)}, f32[10,16,128]{2,1,0:T(8,128)S(1)}, u32[]{:S(2)}, u32[]{:S(2)}) collective-permute-start(f32[10,16,128]{2,1,0:T(8,128)S(1)} %get-tuple-element.23), channel_id=1, source_target_pairs={{0,3},{1,0},{2,1},{3,2},{4,7},{5,4},{6,5},{7,6},{8,11},{9,8},{10,9... | collective-permute-start | bytes 245768 | tf_op jit(solution)/shard_map/ppermute | solution.py:596
  9.9 14.3 %collective-permute-start.4 = (f32[8,40,128]{2,1,0:T(8,128)S(1)}, f32[8,40,128]{2,1,0:T(8,128)S(1)}, u32[]{:S(2)}, u32[]{:S(2)}) collective-permute-start(f32[8,40,128]{2,1,0:T(8,128)S(1)} %get-tuple-element.24.side), channel_id=1, source_target_pairs={{0,16},{16,0},{1,17},{17,1},{2,18},{18,2},{3,19},{19,3},{4,20},{20... | collective-permute-start | bytes 491528 | tf_op jit(solution)/shard_map/ppermute | solution.py:600
  11.5 6.3 %collective-permute-start.5 = (f32[144,128]{1,0:T(8,128)S(1)}, f32[144,128]{1,0:T(8,128)S(1)}, u32[]{:S(2)}, u32[]{:S(2)}) collective-permute-start(f32[144,128]{1,0:T(8,128)S(1)} %get-tuple-element.25), channel_id=1, source_target_pairs={{0,4},{4,8},{8,12},{12,0},{1,5},{5,9},{9,13},{13,1},{2,6},{6,10},{... | collective-permute-start | bytes 221192 | tf_op jit(solution)/shard_map/ppermute | solution.py:596
  13.1 6.4 %collective-permute-start.7 = (f32[144,128]{1,0:T(8,128)S(1)}, f32[144,128]{1,0:T(8,128)S(1)}, u32[]{:S(2)}, u32[]{:S(2)}) collective-permute-start(f32[144,128]{1,0:T(8,128)S(1)} %get-tuple-element.26), channel_id=1, source_target_pairs={{0,12},{4,0},{8,4},{12,8},{1,13},{5,1},{9,5},{13,9},{2,14},{6,2},{... | collective-permute-start | bytes 221192 | tf_op jit(solution)/shard_map/ppermute | solution.py:596
  17.8 5.0 %collective-permute-start.6 = (f32[144,128]{1,0:T(8,128)S(1)}, f32[144,128]{1,0:T(8,128)S(1)}, u32[]{:S(2)}, u32[]{:S(2)}) collective-permute-start(f32[144,128]{1,0:T(8,128)S(1)} %collective-permute-done.5.ylo), channel_id=1, source_target_pairs={{0,16},{16,0},{1,17},{17,1},{2,18},{18,2},{3,19},{19,3},{4,20},{20... | collective-permute-start | bytes 221192 | tf_op jit(solution)/shard_map/ppermute | solution.py:600
  19.5 4.6 %collective-permute-start.8 = (f32[144,128]{1,0:T(8,128)S(1)}, f32[144,128]{1,0:T(8,128)S(1)}, u32[]{:S(2)}, u32[]{:S(2)}) collective-permute-start(f32[144,128]{1,0:T(8,128)S(1)} %collective-permute-done.7.yhi), channel_id=1, source_target_pairs={{0,16},{16,0},{1,17},{17,1},{2,18},{18,2},{3,19},{19,3},{4,20},{20... | collective-permute-start | bytes 221192 | tf_op jit(solution)/shard_map/ppermute | solution.py:600
